TPU v7x, 512 devices: a whole 4x4x16 slice. The times are simulated.
512 devices in a mesh: grp: 16 (over z), voc: 32 (over x, y, core).
Axes of the slice: x: 4, y: 4, z: 16, core: 2. Of those that a mesh axis runs over, the one named last changes fastest.
Arguments:
- hidden_states: bfloat16 [16384, 8192], P('grp', 'voc'), may hold values from -6 to 6
- target_logits: float32 [16384, 16384], P('grp', 'voc'), may hold values from -12 to 240
- labels: int32 [16384, 8], P('grp'), may hold values from 0 to 2047
- down_weight: bfloat16 [8192, 256], P('voc'), may hold values from -0.0625 to 0.0625
- up_weight: bfloat16 [256, 8192], P(None, 'grp'), may hold values from -0.75 to 0.75
- head_weight: bfloat16 [8192, 16384], P('grp', 'voc'), may hold values from -0.0625 to 0.0625
Outputs:
- frame_loss: float32 [32, 16, 256], P('voc', 'grp')
- grad_a: float32 [8192, 256], P('voc')
- grad_b: float32 [256, 8192], P(None, 'grp')
All inputs are finite; a program needn't handle non-finite values.
Results may differ from a plain program's by a relative error of at most 0.0046.
Values may be sent and summed in bfloat16 or wider, within the bound.
A program may use at most 64 MiB of HBM per device.

v0:
```python
import jax
import jax.numpy as jnp
from jax import lax
from jax.sharding import PartitionSpec as P

HEAD = 2


LAM = 0.1


def passed_along(block, axis, distance):
    devices = range(lax.axis_size(axis))
    route = [(i - distance, i) for i in devices if i - distance in devices]
    return lax.ppermute(block, axis, route)


def partner(value, axis, bit):
    mask = 2**bit
    pairs = [(source, source ^ mask) for source in range(lax.axis_size(axis))]
    return lax.ppermute(value, axis, pairs)


def silu_slope(values):
    sigma = jax.nn.sigmoid(values)
    return sigma * (1.0 + values * (1.0 - sigma))


def log_normalize(values):
    top_value = jnp.max(values, -1, keepdims=True)
    return values - top_value - jnp.log(jnp.sum(jnp.exp(values - top_value), -1, keepdims=True))


def inner_rows(left, right):
    return lax.dot_general(
        left, right, (((0,), (0,)), ((), ())), preferred_element_type=jnp.float32
    )


def inner_cols(left, right):
    return lax.dot_general(
        left, right, (((1,), (1,)), ((), ())), preferred_element_type=jnp.float32
    )


def regroup(blocks, bit_total, swapper):
    position = lax.axis_index("voc")
    for bit_number in range(bit_total):
        leading = blocks.shape[:-3]
        slot_count = blocks.shape[-3]
        lower_count = 1 << bit_number
        upper_count = slot_count // (2 * lower_count)
        viewed = blocks.reshape(leading + (upper_count, 2, lower_count) + blocks.shape[-2:])
        bit_axis = len(leading) + 1
        own_bit = position // lower_count % 2
        zero_half = lax.index_in_dim(viewed, 0, bit_axis, keepdims=False)
        one_half = lax.index_in_dim(viewed, 1, bit_axis, keepdims=False)
        kept = jnp.where(own_bit == 0, zero_half, one_half)
        outgoing = jnp.where(own_bit == 0, one_half, zero_half)
        arrived = swapper(outgoing, bit_number)
        low_half = jnp.where(own_bit == 0, kept, arrived)
        high_half = jnp.where(own_bit == 0, arrived, kept)
        blocks = jnp.stack((low_half, high_half), bit_axis).reshape(blocks.shape)
    return blocks


def on_device(hidden_states, target_logits, labels, down_weight, up_weight, head_weight):
    row_count, slice_cols = target_logits.shape
    book_count = labels.shape[1]
    group_count = lax.axis_size("grp")
    per_book = lax.axis_size("voc") // book_count
    bit_total = per_book.bit_length() - 1
    book_width = slice_cols * per_book
    block_rows = row_count // per_book
    position = lax.axis_index("voc")
    book_index = position // per_book
    book_part = position % per_book
    pre_act = lax.psum(
        jnp.dot(hidden_states, down_weight, preferred_element_type=jnp.float32), "voc"
    )
    activation = jax.nn.silu(pre_act).astype(jnp.bfloat16)
    vocab_proj = lax.psum(
        jnp.dot(up_weight, head_weight, preferred_element_type=jnp.float32), "grp"
    ).astype(jnp.bfloat16)
    draft_logits = target_logits + jnp.dot(
        activation, vocab_proj, preferred_element_type=jnp.float32
    )
    incoming = passed_along(target_logits[:HEAD], "grp", -1)
    shifted = jnp.concatenate((target_logits[HEAD:], incoming), 0)
    frame_index = lax.axis_index("grp") * row_count + jnp.arange(row_count)
    live_mask = (frame_index < row_count * group_count - HEAD).astype(jnp.float32)
    paired = jnp.stack((shifted, draft_logits)).reshape(2, per_book, block_rows, slice_cols)
    regrouped = regroup(
        paired, bit_total, lambda piece_data, bit_number: partner(piece_data, "voc", bit_number)
    )
    regrouped = regrouped.transpose(0, 2, 1, 3).reshape(2, block_rows, book_width)
    log_target = log_normalize(regrouped[0])
    log_draft = log_normalize(regrouped[1])
    block_start = book_part * block_rows
    label_ids = lax.dynamic_slice(labels, (block_start, book_index), (block_rows, 1))[:, 0]
    live_rows = lax.dynamic_slice_in_dim(live_mask, block_start, block_rows)
    onehot = (jnp.arange(book_width)[None, :] == label_ids[:, None]).astype(jnp.float32)
    target_prob = jnp.exp(log_target)
    draft_prob = jnp.exp(log_draft)
    divergence = jnp.sum(target_prob * (log_target - log_draft), -1)
    picked = jnp.sum(onehot * log_draft, -1)
    frame_loss = (live_rows * divergence - LAM * picked).reshape(1, 1, block_rows)
    block_grad = (
        live_rows[:, None] * (draft_prob - target_prob) + LAM * (draft_prob - onehot)
    ).astype(jnp.bfloat16)
    returned = block_grad.reshape(block_rows, per_book, slice_cols).transpose(1, 0, 2)
    returned = regroup(
        returned, bit_total, lambda piece_data, bit_number: partner(piece_data, "voc", bit_number)
    )
    logit_grad = returned.reshape(row_count, slice_cols)
    act_part = inner_cols(logit_grad, vocab_proj)
    proj_grad = lax.psum(inner_rows(activation, logit_grad), "grp").astype(jnp.bfloat16)
    up_part = inner_cols(proj_grad, head_weight)
    act_grad = lax.psum(act_part, "voc")
    grad_b = lax.psum(up_part, "voc")
    pre_grad = (act_grad * silu_slope(pre_act)).astype(jnp.bfloat16)
    grad_a = lax.psum(inner_rows(hidden_states, pre_grad), "grp")
    return (frame_loss, grad_a, grad_b)


def solution(mesh):
    in_specs = (
        P("grp", "voc"),
        P("grp", "voc"),
        P("grp", None),
        P("voc", None),
        P(None, "grp"),
        P("grp", "voc"),
    )
    out_specs = (P("voc", "grp", None), P("voc", None), P(None, "grp"))
    return jax.shard_map(
        on_device, mesh=mesh, in_specs=in_specs, out_specs=out_specs, check_vma=False
    )
```

profile of v0, /device:TPU:2, one launch (start us, length us, event | category | flops | bytes accessed | tf_op | source)
XLA Modules:
  0.0 595.0 jit_solution(6902269092445431331)
XLA Ops:
  7.2 0.0 copy-start
  7.2 0.0 copy-start.3
  7.2 0.0 copy-start.4
  7.2 0.0 all-reduce.7.cloned.1.call-start
  7.2 1.0 copy-done
  8.2 2.2 fusion.24
  10.4 0.0 all-reduce.7.cloned.1.call-update
  10.4 0.0 all-reduce.11.cloned.1.call-start
  10.5 0.0 copy-done.3
  10.5 1.3 collective-permute-start
  11.8 0.0 copy-done.4
  11.8 2.0 fusion.25
  13.9 69.8 %all-reduce.12 = bf16[256,512]{1,0:T(8,128)(2,1)S(1)} all-reduce(f32[256,512]{1,0:T(8,128)} %fusion.25), channel_id=1, replica_groups=mesh['grp'=16,'voc'=32] {'grp'}, use_global_device_ids=true, to_apply=%region_1.2 | all-reduce | flops 131072 | bytes 786432 | tf_op jit(solution)/shard_map/psum | solution.py:82
  83.6 1.6 slice.38
  85.3 0.0 collective-permute-done
  85.3 1.8 pad_maximum_fusion.2
  87.0 64.4 %all-reduce.7.cloned.1.call-done = f32[1024,256]{1,0:T(8,128)} async-done(((f32[1024,256]{1,0:T(8,128)}), f32[1024,256]{1,0:T(8,128)}) %all-reduce.7.cloned.1.call-update) | async-done | bytes 1048592 | tf_op jit(solution)/shard_map/psum | solution.py:78
  151.5 2.4 convolution_add_fusion
  153.9 0.0 copy-start.2
  153.9 1.9 select_bitcast_fusion.5
  155.8 0.0 copy-done.2
  155.8 2.0 collective-permute-start.1
  157.9 4.3 collective-permute-done.1
  162.2 3.4 select_bitcast_fusion.4
  165.6 0.4 maximum_bitcast_fusion
  166.1 0.0 copy-start.1
  166.1 0.5 select_bitcast_fusion.2
  166.6 1.5 copy-done.1
  168.1 2.5 collective-permute-start.2
  170.6 0.8 dynamic_slice.7
  171.4 46.4 %collective-permute-done.2 = f32[2,1,2,256,512]{4,3,0,2,1:T(8,128)} collective-permute-done((f32[2,1,2,256,512]{4,3,0,2,1:T(8,128)S(1)}, f32[2,1,2,256,512]{4,3,0,2,1:T(8,128)}, u32[]{:S(2)}, u32[]{:S(2)}) %collective-permute-start.2) | collective-permute-done | bytes 2097184 | tf_op jit(solution)/shard_map/ppermute | solution.py:21
  217.7 3.6 select_bitcast_fusion.1
  221.4 0.5 pad_maximum_fusion
  221.9 0.2 bitcast_reduce_fusion
  222.1 0.2 slice_reduce_fusion
  222.2 0.7 exponential_reduce_fusion.1
  223.0 1.0 multiply_reduce_fusion
  224.0 0.6 multiply_subtract_fusion
  224.6 1.6 fusion.6
  226.2 0.1 fusion.12
  226.2 1.9 collective-permute-start.3
  228.2 1.9 collective-permute-done.3
  230.0 0.1 select_bitcast_fusion.9
  230.2 0.1 maximum_bitcast_fusion.1
  230.3 0.1 fusion.13
  230.3 2.5 collective-permute-start.4
  232.8 13.4 %collective-permute-done.4 = bf16[1,2,256,512]{3,2,1,0:T(8,128)(2,1)S(1)} collective-permute-done((bf16[1,2,256,512]{3,2,1,0:T(8,128)(2,1)S(1)}, bf16[1,2,256,512]{3,2,1,0:T(8,128)(2,1)S(1)}, u32[]{:S(2)}, u32[]{:S(2)}) %collective-permute-start.4) | collective-permute-done | bytes 524320 | tf_op jit(solution)/shard_map/ppermute | solution.py:21
  246.2 0.1 select_bitcast_fusion.7
  246.3 0.0 copy-start.6
  246.3 0.1 pad_maximum_fusion.3
  246.4 1.5 fusion.27
  247.9 0.0 copy-done.6
  247.9 0.5 fusion.23
  248.4 63.2 %all-reduce.13 = bf16[256,512]{1,0:T(8,128)(2,1)S(1)} all-reduce(f32[256,512]{1,0:T(8,128)S(1)} %fusion.23), channel_id=1, replica_groups=mesh['grp'=16,'voc'=32] {'grp'}, use_global_device_ids=true, to_apply=%region_10.11 | all-reduce | flops 131072 | bytes 786432 | tf_op jit(solution)/shard_map/psum | solution.py:117
  311.6 1.1 fusion.26
  312.7 0.0 all-reduce.11.cloned.1.call-update
  312.7 0.0 all-reduce.9.cloned.1.call-start
  312.8 133.0 %all-reduce.11.cloned.1.call-done = (f32[1024,256]{1,0:T(8,128)}, f32[256,512]{1,0:T(8,128)}) async-done(((f32[1024,256]{1,0:T(8,128)}, f32[256,512]{1,0:T(8,128)}), (f32[1024,256]{1,0:T(8,128)}, f32[256,512]{1,0:T(8,128)})) %all-reduce.11.cloned.1.call-update) | async-done | bytes 1572880 | tf_op jit(solution)/shard_map/psum | solution.py:119
  445.8 2.6 convolution_bitcast_fusion
  448.4 0.0 all-reduce.9.cloned.1.call-update
  448.4 137.5 %all-reduce.9.cloned.1.call-done = f32[256,256]{0,1:T(8,128)} async-done(((f32[256,256]{0,1:T(8,128)}), f32[256,256]{0,1:T(8,128)}) %all-reduce.9.cloned.1.call-update) | async-done | bytes 262160 | tf_op jit(solution)/shard_map/psum | solution.py:122
  585.9 1.8 copy.27
  587.6 0.0 copy-done.5
  587.7 0.8 copy.41
  (6 shorter events, 0.0 us)
Async XLA Ops:
  7.2 1.0 copy-start
  7.2 3.3 copy-start.3
  7.2 4.6 copy-start.4
  7.2 144.3 %all-reduce.7.cloned.1.call-start = ((), (), s32[]{:S(2)}) async-start(), calls=%async_computation | async-start | bytes 2097152 | tf_op jit(solution)/shard_map/psum | solution.py:78
  10.4 435.4 %all-reduce.11.cloned.1.call-start = ((), (), s32[]{:S(2)}) async-start(), calls=%async_computation.2 | async-start | bytes 3145728 | tf_op jit(solution)/shard_map/psum | solution.py:119
  10.5 74.8 %collective-permute-start = (f32[2,512]{1,0:T(2,128)S(1)}, f32[2,512]{1,0:T(2,128)S(1)}, u32[]{:S(2)}, u32[]{:S(2)}) collective-permute-start(f32[2,512]{1,0:T(2,128)S(1)} %slice.39), channel_id=1, source_target_pairs={{32,0},{64,32},{96,64},{128,96},{160,128},{192,160},{224,192},{256... | collective-permute-start | bytes 12296 | tf_op jit(solution)/shard_map/ppermute | solution.py:15
  153.9 2.0 copy-start.2
  155.8 6.4 %collective-permute-start.1 = (f32[2,2,1,256,512]{4,3,1,0,2:T(8,128)}, f32[2,2,1,256,512]{4,3,1,0,2:T(8,128)}, u32[]{:S(2)}, u32[]{:S(2)}) collective-permute-start(f32[2,2,1,256,512]{4,3,1,0,2:T(8,128)} %select_bitcast_fusion.5), channel_id=1, source_target_pairs={{0,1},{1,0},{2,3},{3,2},{4,5},{5,4},{6,7},{7,6},{8,9},{9,8},{10,11... | collective-permute-start | bytes 6291464 | tf_op jit(solution)/shard_map/ppermute | solution.py:21
  166.1 2.0 copy-start.1
  168.1 49.7 %collective-permute-start.2 = (f32[2,1,2,256,512]{4,3,0,2,1:T(8,128)S(1)}, f32[2,1,2,256,512]{4,3,0,2,1:T(8,128)}, u32[]{:S(2)}, u32[]{:S(2)}) collective-permute-start(f32[2,1,2,256,512]{4,3,0,2,1:T(8,128)S(1)} %select_bitcast_fusion.2), channel_id=1, source_target_pairs={{0,2},{1,3},{2,0},{3,1},{4,6},{5,7},{6,4},{7,5},{8,10},{9,11},{10,... | collective-permute-start | bytes 6291464 | tf_op jit(solution)/shard_map/ppermute | solution.py:21
  226.2 3.8 collective-permute-start.3
  230.3 15.9 %collective-permute-start.4 = (bf16[1,2,256,512]{3,2,1,0:T(8,128)(2,1)S(1)}, bf16[1,2,256,512]{3,2,1,0:T(8,128)(2,1)S(1)}, u32[]{:S(2)}, u32[]{:S(2)}) collective-permute-start(bf16[1,2,256,512]{3,2,1,0:T(8,128)(2,1)S(1)} %fusion.13), channel_id=1, source_target_pairs={{0,2},{1,3},{2,0},{3,1},{4,6},{5,7},{6,4},{7,5},{8,10},{9,11},{10,... | collective-permute-start | bytes 1572872 | tf_op jit(solution)/shard_map/ppermute | solution.py:21
  246.3 1.6 copy-start.6
  312.7 273.1 %all-reduce.9.cloned.1.call-start = ((), (), s32[]{:S(2)}) async-start(), calls=%async_computation.1 | async-start | bytes 524288 | tf_op jit(solution)/shard_map/psum | solution.py:122
  445.8 141.9 %copy-start.5 = (f32[256,512]{1,0:T(8,128)S(1)}, f32[256,512]{1,0:T(8,128)}, u32[]{:S(2)}) copy-start(f32[256,512]{1,0:T(8,128)} %get-tuple-element.24) | copy-start | bytes 1572868
Sparse Core Ops, SparseCore 0:
  11.2 140.2 all-reduce.6
  312.8 132.9 all-reduce.10
  448.7 137.1 all-reduce.8
where the time goes:
time: 595 us
  waiting for transfers between devices  401 us (67%)
  blocking collectives  133 us (22%)
  other arithmetic  17 us (3%)
  between operations  14.1 us (2%)
  matrix products  12.3 us (2%)
  starting transfers between devices  10.3 us (2%)
  local copies, waits for them, and re-layouts  7.43 us (1%)
    psum x1, waiting for transfers between devices, on_device(): grad_a = lax.psum(inner_rows(hidden_states, pre_grad), 'grp')  137 us
    psum x1, waiting for transfers between devices, on_device(): act_grad = lax.psum(act_part, 'voc')  133 us
    psum x1, blocking collectives, on_device(): lax.psum(jnp.dot(up_weight, head_weight, preferred_element_type=jnp.float...  69.8 us
    ppermute x4, waiting for transfers between devices, partner(): return lax.ppermute(value, axis, pairs)  66 us
    psum x1, waiting for transfers between devices, on_device(): lax.psum(jnp.dot(hidden_states, down_weight, preferred_element_type=jnp.f...  64.4 us
    psum x1, blocking collectives, on_device(): lax.psum(inner_rows(activation, logit_grad), 'grp').astype(jnp.bfloat16)  63.2 us
  transfers between devices with their start and end apart: 8, of which 7 were waited for; matrix products, arithmetic and copies ran while one was open for 1% of the time, Pallas kernels for 0%

commit v1 on v0

v1 whole, which is shorter than its diff:
```python
import functools

import jax
import jax.numpy as jnp
from jax import lax
from jax.experimental import pallas as pl
from jax.experimental.pallas import tpu as pltpu
from jax.sharding import PartitionSpec as P

HEAD = 2
LAM = 0.1
MESH = pl.DeviceIdType.MESH
F32 = jnp.float32
BF16 = jnp.bfloat16
CHUNK = 128
WIRE = {"a": F32, "v": BF16, "b": F32, "p": BF16, "g": F32, "ag": F32, "c": F32, "ac": F32}

PHASES = (
    "halo", "pair_a", "rs_a", "ag_a", "back_a", "s1", "s2", "s3",
    "pair_b", "rs_b", "ag_b", "back_b", "pair_c", "rs_c", "ag_c", "back_c",
) + tuple(
    ring + stage
    for ring in ("v", "p", "g")
    for stage in ("_up", "_down", "_near", "_ahead", "_behind", "_rest")
)
HOP = 4
SEM = {name: number for number, name in enumerate(PHASES)}


def dot_nt(left, right):
    return lax.dot_general(left, right, (((1,), (1,)), ((), ())), preferred_element_type=F32)


def dot_nn(left, right):
    return jnp.dot(left, right, preferred_element_type=F32)


def kernel(
    n_grp, n_voc, n_book,
    h_any, t_any, lab_ref, dw_any, uw_any, hw_any,
    loss_ref, ga_ref, gb_ref,
    h, t, dw, uw, hw, h_t,
    pv, pv_s, pv_o, pv_r, vp,
    pa, pair_a, pa2, rv_a, pre, acts, acts_t,
    labc, ssh, et, ed, statcol, stat, rv_s, comb, grad,
    pp, pp_s, pp_o, pp_r, proj,
    pb, pair_b, pb2, rv_b, pg,
    px, px_s, px_o, px_r, gag,
    pc, pair_c, pc2, rv_c, gcol, gpart,
    in_sem, send_sem, recv_sem,
):
    g = lax.axis_index("grp")
    v = lax.axis_index("voc")
    chips = n_voc // 2
    chip = v // 2
    core = v % 2
    other = 1 - core
    twin = chip * 2 + other
    per_book = n_voc // n_book
    book = v // per_book
    part = v % per_book
    rows, width = ssh.shape
    rank = vp.shape[0]
    half = rows // 2
    a_rows = half // chips
    v_rows = rank // n_grp
    c_rows = rank // chips
    half_w = gb_ref.shape[1] // 2

    loads = [
        pltpu.make_async_copy(uw_any, uw, in_sem.at[0]),
        pltpu.make_async_copy(hw_any, hw, in_sem.at[1]),
        pltpu.make_async_copy(h_any, h, in_sem.at[2]),
        pltpu.make_async_copy(dw_any, dw, in_sem.at[3]),
        pltpu.make_async_copy(t_any, t.at[pl.ds(0, rows)], in_sem.at[4]),
    ]
    for load in loads:
        load.start()

    def z_peer(offset):
        return {"grp": lax.rem(g + offset, n_grp), "voc": v}

    def chip_peer(offset):
        return {"grp": g, "voc": lax.rem(chip + offset, chips) * 2 + core}

    def book_peer(offset):
        return {"grp": g, "voc": book * per_book + lax.rem(part + offset, per_book)}

    barrier = pltpu.get_barrier_semaphore()

    def greet(device):
        pl.semaphore_signal(barrier, inc=1, device_id=device, device_id_type=MESH)

    def loop(count, body):
        def step(index, carry):
            body(index)
            return carry
        lax.fori_loop(0, count, step, 0)

    for hop in range(1, HOP + 1):
        greet(z_peer(hop))
        greet(z_peer(n_grp - hop))
    loop(chips - 1, lambda i: greet(chip_peer(i + 1)))
    greet({"grp": g, "voc": twin})
    greet({"grp": g, "voc": book * per_book + lax.rem(part + 2, per_book) // 2 * 2 + other})

    def remote(src, dst, name, device):
        return pltpu.make_async_remote_copy(
            src_ref=src, dst_ref=dst, send_sem=send_sem.at[SEM[name]],
            recv_sem=recv_sem.at[SEM[name]], device_id=device, device_id_type=MESH,
        )

    def wait_for(ref, name):
        pltpu.make_async_copy(ref, ref, recv_sem.at[SEM[name]]).wait()

    def wait_sent(ref, name):
        pltpu.make_async_copy(ref, ref, send_sem.at[SEM[name]]).wait()

    def ordered(index, count):
        return count // 2 + jnp.where(index % 2 == 0, -(index // 2), (index + 1) // 2)

    def scatter(src, piece, dst, name, peer, me, count):
        def send(index):
            offset = ordered(index, count)
            target = lax.rem(me + offset, count)
            remote(
                src.at[pl.ds(pl.multiple_of(target * piece, piece), piece)],
                dst.at[offset - 1], name, peer(offset),
            ).start()
        loop(count - 1, send)

    def gather(ref, piece, start, name, peer, count):
        def send(index):
            offset = ordered(index, count)
            mine = ref.at[pl.ds(pl.multiple_of(start, piece), piece)]
            remote(mine, mine, name, peer(offset)).start()
        loop(count - 1, send)

    def total(own, ref, count):
        acc = own
        for slot in range(count - 1):
            acc = acc + ref[slot].astype(F32)
        return acc

    def block_of(ref, distance, piece):
        where = lax.rem(g + n_grp + distance, n_grp)
        return ref.at[pl.ds(pl.multiple_of(where * piece, piece), piece)]

    def ring_peer(distance):
        return z_peer(n_grp + distance)

    def ring_scatter(name, src, slots, piece):
        for hop in range(HOP, 0, -1):
            remote(
                block_of(src, hop + HOP, piece), slots.at[hop - 1], name + "_up", ring_peer(hop)
            ).start()
            if hop < HOP:
                remote(
                    block_of(src, -hop - HOP, piece), slots.at[HOP + hop - 1], name + "_down",
                    ring_peer(-hop),
                ).start()
        for hop in range(HOP - 1, 0, -1):
            for way in (1, -1):
                slot = slots.at[2 * HOP - 1 + hop - 1 + (0 if way > 0 else HOP - 1)]
                remote(
                    block_of(src, way * hop, piece), slot, name + "_near", ring_peer(way * hop)
                ).start()

    def ring_relay(name, raw, out, slots, piece):
        first = 4 * HOP - 3
        for way, tag, low, count in ((1, "_up", 0, HOP), (-1, "_down", HOP, HOP - 1)):
            wait_for(slots.at[pl.ds(low, count)], name + tag)
            acc = block_of(raw, way * HOP, piece)[...]
            for slot in range(low, low + count):
                acc = acc + slots[slot].astype(F32)
            side = 0 if way > 0 else 1
            out[side] = acc.astype(out.dtype)
            remote(out.at[side], slots.at[first + side], name + "_near", ring_peer(way * HOP)).start()

    def ring_total(name, raw, slots, piece):
        low, count = 2 * HOP - 1, 2 * HOP
        wait_for(slots.at[pl.ds(low, count)], name + "_near")
        acc = block_of(raw, 0, piece)[...]
        for slot in range(low, low + count):
            acc = acc + slots[slot].astype(F32)
        return acc

    def ring_gather(name, ref, piece):
        mine = block_of(ref, 0, piece)
        for hop in range(HOP, 0, -1):
            for way, tag in ((1, "_ahead"), (-1, "_behind")):
                kind = tag if hop == HOP else "_rest"
                remote(mine, mine, name + kind, ring_peer(way * hop)).start()

    def ring_forward(name, ref, piece):
        for way, tag, last in ((1, "_ahead", HOP), (-1, "_behind", HOP - 1)):
            held = block_of(ref, -way * HOP, piece)
            wait_for(held, name + tag)
            for hop in range(last, 0, -1):
                remote(held, held, name + "_rest", ring_peer(way * hop)).start()

    def ring_done(name, ref, piece):
        wait_for(ref.at[pl.ds(0, (n_grp - 3) * piece)], name + "_rest")

    def ring_sent(name, slots, ref, piece):
        wait_sent(slots.at[pl.ds(0, HOP)], name + "_up")
        wait_sent(slots.at[pl.ds(0, HOP - 1)], name + "_down")
        wait_sent(slots.at[pl.ds(0, 2 * HOP)], name + "_near")
        wait_sent(ref.at[pl.ds(0, piece)], name + "_ahead")
        wait_sent(ref.at[pl.ds(0, piece)], name + "_behind")
        wait_sent(ref.at[pl.ds(0, (n_grp - 3) * piece)], name + "_rest")

    def turn(src, dst):
        def body(index):
            at = pl.ds(pl.multiple_of(index * 256, 256), 256)
            dst[:, at] = src[at, :].T
        loop(rows // 256, body)

    loads[0].wait()
    loads[1].wait()
    pv[...] = dot_nn(uw[...], hw[...])
    pv_s[...] = pv[...].astype(pv_s.dtype)
    pl.semaphore_wait(barrier, 2 * HOP + chips - 1 + 2)
    ring_scatter("v", pv_s, pv_r, v_rows)
    remote(
        t_any.at[pl.ds(0, 8)], t.at[pl.ds(rows, 8)], "halo", ring_peer(-1)
    ).start()
    loads[2].wait()
    loads[3].wait()

    def first(index):
        at = pl.ds(pl.multiple_of(index * 256, 256), 256)
        value = dot_nn(h[at, :], dw[...])
        pa[at, :] = value
    loop(rows // 256, first)

    mine_half = pl.ds(pl.multiple_of(core * half, half), half)
    twin_half = pl.ds(pl.multiple_of(other * half, half), half)
    twin_id = {"grp": g, "voc": twin}
    remote(pa.at[twin_half], pair_a, "pair_a", twin_id).start()
    wait_for(pair_a, "pair_a")
    pa2[...] = (pa[mine_half, :] + pair_a[...]).astype(pa2.dtype)
    scatter(pa2, a_rows, rv_a, "rs_a", chip_peer, chip, chips)

    turn(h, h_t)
    loads[4].wait()
    ring_relay("v", pv, pv_o, pv_r, v_rows)
    wait_for(t.at[pl.ds(rows, 8)], "halo")
    t[pl.ds(rows, 8), :] = jnp.where(g == n_grp - 1, 0.0, t[pl.ds(rows, 8), :])

    def target_pass(index):
        start = pl.multiple_of(index * CHUNK, CHUNK)
        at = pl.ds(start, CHUNK)
        block = t[pl.ds(start, CHUNK + 8), :]
        shifted = pltpu.roll(block, CHUNK + 8 - HEAD, 0)[:CHUNK]
        top = jnp.max(shifted, -1, keepdims=True)
        low = shifted - top
        expo = jnp.exp(low)
        ssh[at, :] = low
        et[at, :] = expo
        norm = jnp.sum(expo, -1, keepdims=True)
        lane = lax.broadcasted_iota(jnp.int32, (CHUNK, 128), 1)
        statcol[at, :] = jnp.where(lane == 0, top, jnp.where(lane == 1, norm, 0.0))
        ids = lab_ref[at, :].astype(F32)
        which = lax.broadcasted_iota(jnp.int32, ids.shape, 1)
        label = jnp.sum(jnp.where(which == book, ids, 0.0), -1, keepdims=True)
        labc[at, :] = jnp.broadcast_to(label - (part * width).astype(F32), (CHUNK, 128))
    loop(rows // CHUNK, target_pass)
    comb[...] = jnp.zeros_like(comb)

    ring_own = pl.ds(pl.multiple_of(g * v_rows, v_rows), v_rows)
    vp[ring_own, :] = ring_total("v", pv, pv_r, v_rows).astype(BF16)
    ring_gather("v", vp, v_rows)

    a_start = chip * a_rows
    own_a = pl.ds(pl.multiple_of(a_start, a_rows), a_rows)
    wait_for(rv_a, "rs_a")
    pre_own = total(pa2[own_a, :].astype(F32), rv_a, chips)
    pre[...] = pre_own
    acts_at = core * half + a_start
    acts[pl.ds(pl.multiple_of(acts_at, a_rows), a_rows), :] = (
        pre_own / (1.0 + jnp.exp(-pre_own))
    ).astype(BF16)
    gather(acts, a_rows, acts_at, "ag_a", chip_peer, chips)
    ring_forward("v", vp, v_rows)

    wait_for(acts.at[pl.ds(0, (chips - 1) * a_rows)], "ag_a")
    remote(acts.at[mine_half], acts.at[mine_half], "back_a", twin_id).start()

    wait_for(acts.at[twin_half], "back_a")
    turn(acts, acts_t)
    ring_done("v", vp, v_rows)

    def label_mask(at):
        labels = labc[at, :]
        col = lax.broadcasted_iota(jnp.int32, (CHUNK, 128), 1).astype(F32)
        return jnp.concatenate([labels == col + 128.0 * k for k in range(width // 128)], 1)

    def draft_pass(index):
        start = pl.multiple_of(index * CHUNK, CHUNK)
        at = pl.ds(start, CHUNK)
        draft = t[at, :] + dot_nn(acts[at, :], vp[...])
        top = jnp.max(draft, -1, keepdims=True)
        low = draft - top
        expo = jnp.exp(low)
        ed[at, :] = expo
        norm = jnp.sum(expo, -1, keepdims=True)
        cross = jnp.sum(et[at, :] * (ssh[at, :] - low), -1, keepdims=True)
        picked = jnp.sum(jnp.where(label_mask(at), draft, 0.0), -1, keepdims=True)
        lane = lax.broadcasted_iota(jnp.int32, (CHUNK, 128), 1)
        cols = statcol[at, :]
        cols = jnp.where(lane == 2, top, cols)
        cols = jnp.where(lane == 3, norm, cols)
        cols = jnp.where(lane == 4, cross, cols)
        cols = jnp.where(lane == 5, picked, cols)
        stat[:, at] = cols.T[:8]
    loop(rows // CHUNK, draft_pass)

    for offset in range(1, per_book):
        remote(stat, rv_s.at[offset - 1], f"s{offset}", book_peer(offset)).start()
    for offset in range(1, per_book):
        wait_for(rv_s.at[offset - 1], f"s{offset}")

    blocks = [stat[...]] + [rv_s[k] for k in range(per_book - 1)]

    def row(block, k):
        return block[k:k + 1, :]

    top_t = functools.reduce(jnp.maximum, [row(b, 0) for b in blocks])
    top_d = functools.reduce(jnp.maximum, [row(b, 2) for b in blocks])
    fac_t = [jnp.exp(row(b, 0) - top_t) for b in blocks]
    fac_d = [jnp.exp(row(b, 2) - top_d) for b in blocks]
    sum_t = sum(row(b, 1) * f for b, f in zip(blocks, fac_t))
    sum_d = sum(row(b, 3) * f for b, f in zip(blocks, fac_d))
    cross = sum(
        f * (row(b, 4) + row(b, 1) * ((row(b, 0) - top_t) - (row(b, 2) - top_d)))
        for b, f in zip(blocks, fac_t)
    )
    picked = sum(row(b, 5) for b in blocks) - top_d - jnp.log(sum_d)
    frame = g * rows + lax.broadcasted_iota(jnp.int32, (1, rows), 1)
    live = (frame < rows * n_grp - HEAD).astype(F32)
    diverge = cross / sum_t - jnp.log(sum_t) + jnp.log(sum_d)
    comb[0:1, :] = (live + LAM) * fac_d[0] / sum_d
    comb[1:2, :] = live * fac_t[0] / sum_t
    comb[2:3, :] = live * diverge - LAM * picked
    block_rows = rows // per_book
    loss_ref[0] = comb[2:3, pl.ds(pl.multiple_of(part * block_rows, block_rows), block_rows)]

    def grad_pass(index):
        at = pl.ds(pl.multiple_of(index * CHUNK, CHUNK), CHUNK)
        cols = comb[:, at].T
        value = ed[at, :] * cols[:, 0:1] - et[at, :] * cols[:, 1:2]
        value = value - jnp.where(label_mask(at), LAM, 0.0)
        grad[at, :] = value.astype(BF16)
    loop(rows // CHUNK, grad_pass)

    pp[...] = dot_nn(acts_t[...], grad[...])
    pp_s[...] = pp[...].astype(pp_s.dtype)
    ring_scatter("p", pp_s, pp_r, v_rows)

    def back(index):
        at = pl.ds(pl.multiple_of(index * 256, 256), 256)
        value = dot_nt(grad[at, :], vp[...])
        pb[at, :] = value
    loop(rows // 256, back)
    remote(pb.at[twin_half], pair_b, "pair_b", twin_id).start()
    wait_for(pair_b, "pair_b")
    pb2[...] = (pb[mine_half, :] + pair_b[...]).astype(pb2.dtype)
    scatter(pb2, a_rows, rv_b, "rs_b", chip_peer, chip, chips)
    ring_relay("p", pp, pp_o, pp_r, v_rows)
    proj[ring_own, :] = ring_total("p", pp, pp_r, v_rows).astype(BF16)
    ring_gather("p", proj, v_rows)
    wait_for(rv_b, "rs_b")
    act_grad = total(pb2[own_a, :].astype(F32), rv_b, chips)
    sigma = 1.0 / (1.0 + jnp.exp(-pre[...]))
    slope = sigma * (1.0 + pre[...] * (1.0 - sigma))
    pg[pl.ds(pl.multiple_of(acts_at, a_rows), a_rows), :] = (act_grad * slope).astype(BF16)
    gather(pg, a_rows, acts_at, "ag_b", chip_peer, chips)

    ring_forward("p", proj, v_rows)

    wait_for(pg.at[pl.ds(0, (chips - 1) * a_rows)], "ag_b")
    remote(pg.at[mine_half], pg.at[mine_half], "back_b", twin_id).start()
    wait_for(pg.at[twin_half], "back_b")
    px[...] = dot_nn(h_t[...], pg[...])
    px_s[...] = px[...].astype(px_s.dtype)
    ring_scatter("g", px_s, px_r, v_rows)

    ring_done("p", proj, v_rows)
    up = dot_nt(proj[...], hw[...])
    for side in range(2):
        pc[side] = up[:, side * half_w:(side + 1) * half_w]
    remote(pc.at[other], pair_c, "pair_c", twin_id).start()
    wait_for(pair_c, "pair_c")
    pc2[...] = (pc[core] + pair_c[...]).astype(pc2.dtype)
    scatter(pc2, c_rows, rv_c, "rs_c", chip_peer, chip, chips)

    ring_relay("g", px, px_o, px_r, v_rows)
    gag[ring_own, :] = ring_total("g", px, px_r, v_rows).astype(gag.dtype)
    ring_gather("g", gag, v_rows)

    own_c = pl.ds(pl.multiple_of(chip * c_rows, c_rows), c_rows)
    wait_for(rv_c, "rs_c")
    gcol[own_c, :] = total(pc2[own_c, :].astype(F32), rv_c, chips).astype(gcol.dtype)
    gather(gcol, c_rows, chip * c_rows, "ag_c", chip_peer, chips)
    ring_forward("g", gag, v_rows)
    wait_for(gcol.at[pl.ds(0, (chips - 1) * c_rows)], "ag_c")
    remote(gcol, gpart, "back_c", twin_id).start()

    ring_done("g", gag, v_rows)
    ga_ref[...] = gag[...].astype(F32)
    wait_for(gpart, "back_c")

    mine = gcol[...].astype(F32)
    theirs = gpart[...].astype(F32)
    gb_ref[:, :half_w] = jnp.where(core == 0, mine, theirs)
    gb_ref[:, half_w:] = jnp.where(core == 0, theirs, mine)

    wait_sent(t.at[pl.ds(rows, 8)], "halo")
    wait_sent(pair_a, "pair_a")
    wait_sent(rv_a, "rs_a")
    wait_sent(acts.at[pl.ds(0, (chips - 1) * a_rows)], "ag_a")
    wait_sent(acts.at[mine_half], "back_a")
    ring_sent("v", pv_r, vp, v_rows)
    for offset in range(1, per_book):
        wait_sent(stat, f"s{offset}")
    wait_sent(pair_b, "pair_b")
    wait_sent(rv_b, "rs_b")
    wait_sent(pg.at[pl.ds(0, (chips - 1) * a_rows)], "ag_b")
    wait_sent(pg.at[mine_half], "back_b")
    ring_sent("p", pp_r, proj, v_rows)
    ring_sent("g", px_r, gag, v_rows)
    wait_sent(pair_c, "pair_c")
    wait_sent(rv_c, "rs_c")
    wait_sent(gcol.at[pl.ds(0, (chips - 1) * c_rows)], "ag_c")
    wait_sent(gcol, "back_c")


def on_device(n_grp, n_voc, hidden_states, target_logits, labels, down_weight, up_weight, head_weight):
    rows, width = target_logits.shape
    n_book = labels.shape[1]
    per_book = n_voc // n_book
    deep = hidden_states.shape[1]
    rank = up_weight.shape[0]
    span = up_weight.shape[1]
    chips = n_voc // 2
    half = rows // 2
    a_rows = half // chips
    v_rows = rank // n_grp
    c_rows = rank // chips
    half_w = span // 2
    vm = pltpu.VMEM
    w = WIRE
    scratch = [
        vm((rows, deep), BF16), vm((rows + 8, width), F32), vm((deep, rank), BF16),
        vm((rank, span), BF16), vm((span, width), BF16), vm((deep, rows), BF16),
        vm((rank, width), F32), vm((rank, width), w["v"]), vm((2, v_rows, width), w["v"]),
        vm((4 * HOP - 1, v_rows, width), w["v"]), vm((rank, width), BF16),
        vm((rows, rank), F32), vm((half, rank), F32),
        vm((half, rank), w["a"]), vm((chips - 1, a_rows, rank), w["a"]), vm((a_rows, rank), F32),
        vm((rows, rank), BF16), vm((rank, rows), BF16),
        vm((rows, 128), F32), vm((rows, width), F32), vm((rows, width), F32),
        vm((rows, width), F32), vm((rows, 128), F32), vm((8, rows), F32),
        vm((per_book - 1, 8, rows), F32), vm((128, rows), F32), vm((rows, width), BF16),
        vm((rank, width), F32), vm((rank, width), w["p"]), vm((2, v_rows, width), w["p"]),
        vm((4 * HOP - 1, v_rows, width), w["p"]), vm((rank, width), BF16),
        vm((rows, rank), F32), vm((half, rank), F32),
        vm((half, rank), w["b"]), vm((chips - 1, a_rows, rank), w["b"]), vm((rows, rank), BF16),
        vm((deep, rank), F32), vm((deep, rank), w["g"]), vm((2, v_rows, rank), w["g"]),
        vm((4 * HOP - 1, v_rows, rank), w["g"]), vm((deep, rank), w["ag"]),
        vm((2, rank, half_w), F32), vm((rank, half_w), F32),
        vm((rank, half_w), w["c"]), vm((chips - 1, c_rows, half_w), w["c"]), vm((rank, half_w), w["ac"]),
        vm((rank, half_w), w["ac"]),
        pltpu.SemaphoreType.DMA((5,)),
        pltpu.SemaphoreType.DMA((len(PHASES),)),
        pltpu.SemaphoreType.DMA((len(PHASES),)),
    ]
    hbm = pl.BlockSpec(memory_space=pl.ANY)
    vmem = pl.BlockSpec(memory_space=pltpu.VMEM)
    return pl.pallas_call(
        functools.partial(kernel, n_grp, n_voc, n_book),
        out_shape=(
            jax.ShapeDtypeStruct((1, 1, rows // per_book), F32),
            jax.ShapeDtypeStruct((deep, rank), F32),
            jax.ShapeDtypeStruct((rank, span), F32),
        ),
        in_specs=[hbm, hbm, vmem, hbm, hbm, hbm],
        out_specs=(vmem, vmem, vmem),
        scratch_shapes=scratch,
        compiler_params=pltpu.CompilerParams(
            collective_id=0, has_side_effects=True, vmem_limit_bytes=60 * 1024 * 1024
        ),
    )(hidden_states, target_logits, labels, down_weight, up_weight, head_weight)


def solution(mesh):
    in_specs = (
        P("grp", "voc"),
        P("grp", "voc"),
        P("grp", None),
        P("voc", None),
        P(None, "grp"),
        P("grp", "voc"),
    )
    out_specs = (P("voc", "grp", None), P("voc", None), P(None, "grp"))
    return jax.shard_map(
        functools.partial(on_device, mesh.shape["grp"], mesh.shape["voc"]),
        mesh=mesh, in_specs=in_specs, out_specs=out_specs, check_vma=False,
    )
```

time: 595 us -> 95.6 us (0.16)
  waiting for transfers between devices: 401 us -> 0 us
  blocking collectives: 133 us -> 0 us
  Pallas kernels: 0 us -> 88.1 us
  other arithmetic: 17 us -> 0 us
  between operations: 14.1 us -> 0.64 us
  matrix products: 12.3 us -> 0 us
  starting transfers between devices: 10.3 us -> 0 us
    psum x3 -> x0, waiting for transfers between devices: 335 us -> none  [the longest x1 137 us: on_device(): grad_a = lax.psum(inner_rows(hidden_states, pre_grad), 'grp')]
    psum x2 -> x0, blocking collectives: 133 us -> none  [the longest x1 69.8 us: on_device(): lax.psum(jnp.dot(up_weight, head_weight, preferred_element_type=jnp.float...]
    pallas_call x0 -> x1, Pallas kernels: none -> 88.1 us  [on_device(): pl.pallas_call(functools.partial(kernel, n_grp, n_voc, n_book), out_shape...]
    ppermute x5 -> x0, waiting for transfers between devices: 66 us -> none  [the longest x4 66 us: partner(): return lax.ppermute(value, axis, pairs)]
    dot_general x7 -> x0, matrix products: 12.3 us -> none  [the longest x2 3.06 us: inner_rows(): lax.dot_general(left, right, (((0,), (0,)), ((), ())), preferred_element_...]
    ppermute x5 -> x0, starting transfers between devices: 10.2 us -> none  [the longest x4 8.86 us: partner(): return lax.ppermute(value, axis, pairs)]
    another operation x8 -> x0, other arithmetic: 8.38 us -> none  [the longest x6 7.84 us: regroup(): blocks = jnp.stack((low_half, high_half), bit_axis).reshape(blocks.shape)]
  transfers between devices with their start and end apart: 8 -> 0, of which waited for: 7 -> 0; matrix products, arithmetic and copies ran while one was open for 1% -> 0% of each run, Pallas kernels for 0% -> 0%
where the time goes in v1:
time: 95.6 us; the launch traced here: 95.3 us
  Pallas kernels  88.1 us (92%)
  local copies, waits for them, and re-layouts  6.52 us (7%)
    pallas_call x1, Pallas kernels, on_device(): pl.pallas_call(functools.partial(kernel, n_grp, n_voc, n_book), out_shape...  88.1 us
    unnamed x4, local copies, waits for them, and re-layouts  6.52 us

profile of v1, /device:TPU:2, one launch (start us, length us, event | category | flops | bytes accessed | tf_op | source)
XLA Modules:
  0.0 95.3 jit_solution(6552031449043453563)
XLA Ops:
  0.6 1.8 %copy.9.lab_ref = s32[1024,8]{1,0:T(8,128)} copy(s32[1024,8]{0,1:T(8,128)} %param.8) | data formatting | bytes 65536 | tf_op args[2]
  2.4 88.1 %shard_map.85 = (f32[1,1,256]{2,1,0:T(1,128)}, f32[256,256]{1,0:T(8,128)}, f32[256,512]{1,0:T(8,128)}) custom-call(bf16[1024,256]{1,0:T(8,128)(2,1)} %h_any.1, f32[1024,512]{1,0:T(8,128)} %t_any.1, s32[1024,8]{1,0:T(8,128)} %copy.9.lab_ref, bf16[256,256]{1,0:T(8,128)(2,1)} %dw_any.1, bf16[256,512]{1,0:T(8,128)(2,1)} %uw_any.1, bf16[512,512]{1,0:T(8,128)(2,1)} %hw_any.1), custom_call_target="tpu_custom_call" | custom-call | tf_op jit(solution)/shard_map/pallas_call | solution.py:480
  90.5 1.2 %copy.13 = f32[1,1,256]{2,1,0:T(1,128)} copy(f32[1,1,256]{2,1,0:T(1,128)} %get-tuple-element.6) | data formatting | bytes 2048
  91.7 1.7 %copy.14 = f32[256,256]{1,0:T(8,128)} copy(f32[256,256]{1,0:T(8,128)} %get-tuple-element.7) | data formatting | bytes 524288
  93.4 1.9 %copy.15 = f32[256,512]{1,0:T(8,128)} copy(f32[256,512]{1,0:T(8,128)} %get-tuple-element.8) | data formatting | bytes 1048576

commit v2 on v1

--- a/solution.py
+++ b/solution.py
@@ -13,15 +13,18 @@
 F32 = jnp.float32
 BF16 = jnp.bfloat16
 CHUNK = 128
-WIRE = {"a": F32, "v": BF16, "b": F32, "p": BF16, "g": F32, "ag": F32, "c": F32, "ac": F32}
+WIRE = {
+    "a": F32, "b": F32, "c": BF16, "v": BF16, "vn": BF16, "vx": F32,
+    "p": BF16, "pn": BF16, "px": BF16, "g": BF16, "gn": BF16, "gx": BF16, "ga": F32,
+}
 
 PHASES = (
     "halo", "pair_a", "rs_a", "ag_a", "back_a", "s1", "s2", "s3",
-    "pair_b", "rs_b", "ag_b", "back_b", "pair_c", "rs_c", "ag_c", "back_c",
+    "pair_b", "rs_b", "ag_b", "back_b", "rs_c", "ag_c",
 ) + tuple(
     ring + stage
     for ring in ("v", "p", "g")
-    for stage in ("_up", "_down", "_near", "_ahead", "_behind", "_rest")
+    for stage in ("_up", "_down", "_near", "_far", "_ahead", "_behind", "_rest")
 )
 HOP = 4
 SEM = {name: number for number, name in enumerate(PHASES)}
@@ -37,16 +40,16 @@
 
 def kernel(
     n_grp, n_voc, n_book,
-    h_any, t_any, lab_ref, dw_any, uw_any, hw_any,
+    h_any, t_any, lab_any, dw_any, uw_any, hw_any,
     loss_ref, ga_ref, gb_ref,
-    h, t, dw, uw, hw, h_t,
-    pv, pv_s, pv_o, pv_r, vp,
+    h, t, lab, dw, uw, hw, h_t,
+    pv, pv_s, pv_o, pv_f, pv_n, pv_r, vp,
     pa, pair_a, pa2, rv_a, pre, acts, acts_t,
     labc, ssh, et, ed, statcol, stat, rv_s, comb, grad,
-    pp, pp_s, pp_o, pp_r, proj,
+    pp, pp_s, pp_o, pp_f, pp_n, pp_r, proj,
     pb, pair_b, pb2, rv_b, pg,
-    px, px_s, px_o, px_r, gag,
-    pc, pair_c, pc2, rv_c, gcol, gpart,
+    px, px_s, px_o, px_f, px_n, px_r, gag,
+    pc, pc_s, rv_c, gall,
     in_sem, send_sem, recv_sem,
 ):
     g = lax.axis_index("grp")
@@ -65,7 +68,7 @@
     a_rows = half // chips
     v_rows = rank // n_grp
     c_rows = rank // chips
-    half_w = gb_ref.shape[1] // 2
+    half_w = gb_ref.shape[2]
 
     loads = [
         pltpu.make_async_copy(uw_any, uw, in_sem.at[0]),
@@ -73,6 +76,7 @@
         pltpu.make_async_copy(h_any, h, in_sem.at[2]),
         pltpu.make_async_copy(dw_any, dw, in_sem.at[3]),
         pltpu.make_async_copy(t_any, t.at[pl.ds(0, rows)], in_sem.at[4]),
+        pltpu.make_async_copy(lab_any, lab, in_sem.at[5]),
     ]
     for load in loads:
         load.start()
@@ -82,6 +86,9 @@
 
     def chip_peer(offset):
         return {"grp": g, "voc": lax.rem(chip + offset, chips) * 2 + core}
+
+    def voc_peer(offset):
+        return {"grp": g, "voc": lax.rem(v + offset, n_voc)}
 
     def book_peer(offset):
         return {"grp": g, "voc": book * per_book + lax.rem(part + offset, per_book)}
@@ -100,9 +107,7 @@
     for hop in range(1, HOP + 1):
         greet(z_peer(hop))
         greet(z_peer(n_grp - hop))
-    loop(chips - 1, lambda i: greet(chip_peer(i + 1)))
-    greet({"grp": g, "voc": twin})
-    greet({"grp": g, "voc": book * per_book + lax.rem(part + 2, per_book) // 2 * 2 + other})
+    loop(n_voc - 1, lambda i: greet(voc_peer(i + 1)))
 
     def remote(src, dst, name, device):
         return pltpu.make_async_remote_copy(
@@ -149,7 +154,7 @@
     def ring_peer(distance):
         return z_peer(n_grp + distance)
 
-    def ring_scatter(name, src, slots, piece):
+    def ring_scatter(name, raw, src, slots, near, piece):
         for hop in range(HOP, 0, -1):
             remote(
                 block_of(src, hop + HOP, piece), slots.at[hop - 1], name + "_up", ring_peer(hop)
@@ -161,13 +166,13 @@
                 ).start()
         for hop in range(HOP - 1, 0, -1):
             for way in (1, -1):
-                slot = slots.at[2 * HOP - 1 + hop - 1 + (0 if way > 0 else HOP - 1)]
+                slot = near.at[hop - 1 + (0 if way > 0 else HOP - 1)]
+                origin = raw if near.dtype == raw.dtype else src
                 remote(
-                    block_of(src, way * hop, piece), slot, name + "_near", ring_peer(way * hop)
+                    block_of(origin, way * hop, piece), slot, name + "_near", ring_peer(way * hop)
                 ).start()
 
-    def ring_relay(name, raw, out, slots, piece):
-        first = 4 * HOP - 3
+    def ring_relay(name, raw, out, far, slots, piece):
         for way, tag, low, count in ((1, "_up", 0, HOP), (-1, "_down", HOP, HOP - 1)):
             wait_for(slots.at[pl.ds(low, count)], name + tag)
             acc = block_of(raw, way * HOP, piece)[...]
@@ -175,15 +180,15 @@
                 acc = acc + slots[slot].astype(F32)
             side = 0 if way > 0 else 1
             out[side] = acc.astype(out.dtype)
-            remote(out.at[side], slots.at[first + side], name + "_near", ring_peer(way * HOP)).start()
-
-    def ring_total(name, raw, slots, piece):
-        low, count = 2 * HOP - 1, 2 * HOP
-        wait_for(slots.at[pl.ds(low, count)], name + "_near")
+            remote(out.at[side], far.at[side], name + "_far", ring_peer(way * HOP)).start()
+
+    def ring_total(name, raw, far, near, piece):
+        wait_for(near, name + "_near")
         acc = block_of(raw, 0, piece)[...]
-        for slot in range(low, low + count):
-            acc = acc + slots[slot].astype(F32)
-        return acc
+        for slot in range(2 * HOP - 2):
+            acc = acc + near[slot].astype(F32)
+        wait_for(far, name + "_far")
+        return acc + far[0].astype(F32) + far[1].astype(F32)
 
     def ring_gather(name, ref, piece):
         mine = block_of(ref, 0, piece)
@@ -202,10 +207,11 @@
     def ring_done(name, ref, piece):
         wait_for(ref.at[pl.ds(0, (n_grp - 3) * piece)], name + "_rest")
 
-    def ring_sent(name, slots, ref, piece):
+    def ring_sent(name, far, slots, near, ref, piece):
         wait_sent(slots.at[pl.ds(0, HOP)], name + "_up")
         wait_sent(slots.at[pl.ds(0, HOP - 1)], name + "_down")
-        wait_sent(slots.at[pl.ds(0, 2 * HOP)], name + "_near")
+        wait_sent(near, name + "_near")
+        wait_sent(far, name + "_far")
         wait_sent(ref.at[pl.ds(0, piece)], name + "_ahead")
         wait_sent(ref.at[pl.ds(0, piece)], name + "_behind")
         wait_sent(ref.at[pl.ds(0, (n_grp - 3) * piece)], name + "_rest")
@@ -220,31 +226,36 @@
     loads[1].wait()
     pv[...] = dot_nn(uw[...], hw[...])
     pv_s[...] = pv[...].astype(pv_s.dtype)
-    pl.semaphore_wait(barrier, 2 * HOP + chips - 1 + 2)
-    ring_scatter("v", pv_s, pv_r, v_rows)
+    pl.semaphore_wait(barrier, 2 * HOP + n_voc - 1)
+    ring_scatter("v", pv, pv_s, pv_r, pv_n, v_rows)
     remote(
         t_any.at[pl.ds(0, 8)], t.at[pl.ds(rows, 8)], "halo", ring_peer(-1)
     ).start()
     loads[2].wait()
     loads[3].wait()
 
-    def first(index):
-        at = pl.ds(pl.multiple_of(index * 256, 256), 256)
-        value = dot_nn(h[at, :], dw[...])
-        pa[at, :] = value
-    loop(rows // 256, first)
-
     mine_half = pl.ds(pl.multiple_of(core * half, half), half)
     twin_half = pl.ds(pl.multiple_of(other * half, half), half)
     twin_id = {"grp": g, "voc": twin}
+
+    def half_dots(dst, start, left, dot, right):
+        def body(index):
+            at = pl.ds(pl.multiple_of(start + index * 256, 256), 256)
+            dst[at, :] = dot(left[at, :], right[...])
+        loop(half // 256, body)
+
+    half_dots(pa, other * half, h, dot_nn, dw)
+
     remote(pa.at[twin_half], pair_a, "pair_a", twin_id).start()
+    half_dots(pa, core * half, h, dot_nn, dw)
     wait_for(pair_a, "pair_a")
     pa2[...] = (pa[mine_half, :] + pair_a[...]).astype(pa2.dtype)
     scatter(pa2, a_rows, rv_a, "rs_a", chip_peer, chip, chips)
 
     turn(h, h_t)
     loads[4].wait()
-    ring_relay("v", pv, pv_o, pv_r, v_rows)
+    loads[5].wait()
+    ring_relay("v", pv, pv_o, pv_f, pv_r, v_rows)
     wait_for(t.at[pl.ds(rows, 8)], "halo")
     t[pl.ds(rows, 8), :] = jnp.where(g == n_grp - 1, 0.0, t[pl.ds(rows, 8), :])
 
@@ -261,15 +272,16 @@
         norm = jnp.sum(expo, -1, keepdims=True)
         lane = lax.broadcasted_iota(jnp.int32, (CHUNK, 128), 1)
         statcol[at, :] = jnp.where(lane == 0, top, jnp.where(lane == 1, norm, 0.0))
-        ids = lab_ref[at, :].astype(F32)
-        which = lax.broadcasted_iota(jnp.int32, ids.shape, 1)
-        label = jnp.sum(jnp.where(which == book, ids, 0.0), -1, keepdims=True)
-        labc[at, :] = jnp.broadcast_to(label - (part * width).astype(F32), (CHUNK, 128))
+        ids = lab[:, at].astype(F32)
+        which = lax.broadcasted_iota(jnp.int32, ids.shape, 0)
+        label = jnp.sum(jnp.where(which == book, ids, 0.0), 0, keepdims=True)
+        label = label - (part * width).astype(F32)
+        labc[at, :] = jnp.broadcast_to(label, (CHUNK, CHUNK)).T
     loop(rows // CHUNK, target_pass)
     comb[...] = jnp.zeros_like(comb)
 
     ring_own = pl.ds(pl.multiple_of(g * v_rows, v_rows), v_rows)
-    vp[ring_own, :] = ring_total("v", pv, pv_r, v_rows).astype(BF16)
+    vp[ring_own, :] = ring_total("v", pv, pv_f, pv_n, v_rows).astype(BF16)
     ring_gather("v", vp, v_rows)
 
     a_start = chip * a_rows
@@ -287,8 +299,6 @@
     wait_for(acts.at[pl.ds(0, (chips - 1) * a_rows)], "ag_a")
     remote(acts.at[mine_half], acts.at[mine_half], "back_a", twin_id).start()
 
-    wait_for(acts.at[twin_half], "back_a")
-    turn(acts, acts_t)
     ring_done("v", vp, v_rows)
 
     def label_mask(at):
@@ -314,10 +324,14 @@
         cols = jnp.where(lane == 4, cross, cols)
         cols = jnp.where(lane == 5, picked, cols)
         stat[:, at] = cols.T[:8]
-    loop(rows // CHUNK, draft_pass)
+    steps = half // CHUNK
+    loop(steps, lambda index: draft_pass(core * steps + index))
+    wait_for(acts.at[twin_half], "back_a")
+    loop(steps, lambda index: draft_pass(other * steps + index))
 
     for offset in range(1, per_book):
         remote(stat, rv_s.at[offset - 1], f"s{offset}", book_peer(offset)).start()
+    turn(acts, acts_t)
     for offset in range(1, per_book):
         wait_for(rv_s.at[offset - 1], f"s{offset}")
 
@@ -356,20 +370,15 @@
 
     pp[...] = dot_nn(acts_t[...], grad[...])
     pp_s[...] = pp[...].astype(pp_s.dtype)
-    ring_scatter("p", pp_s, pp_r, v_rows)
-
-    def back(index):
-        at = pl.ds(pl.multiple_of(index * 256, 256), 256)
-        value = dot_nt(grad[at, :], vp[...])
-        pb[at, :] = value
-    loop(rows // 256, back)
+    ring_scatter("p", pp, pp_s, pp_r, pp_n, v_rows)
+
+    half_dots(pb, other * half, grad, dot_nt, vp)
     remote(pb.at[twin_half], pair_b, "pair_b", twin_id).start()
+    half_dots(pb, core * half, grad, dot_nt, vp)
     wait_for(pair_b, "pair_b")
     pb2[...] = (pb[mine_half, :] + pair_b[...]).astype(pb2.dtype)
     scatter(pb2, a_rows, rv_b, "rs_b", chip_peer, chip, chips)
-    ring_relay("p", pp, pp_o, pp_r, v_rows)
-    proj[ring_own, :] = ring_total("p", pp, pp_r, v_rows).astype(BF16)
-    ring_gather("p", proj, v_rows)
+    ring_relay("p", pp, pp_o, pp_f, pp_r, v_rows)
     wait_for(rv_b, "rs_b")
     act_grad = total(pb2[own_a, :].astype(F32), rv_b, chips)
     sigma = 1.0 / (1.0 + jnp.exp(-pre[...]))
@@ -377,6 +386,8 @@
     pg[pl.ds(pl.multiple_of(acts_at, a_rows), a_rows), :] = (act_grad * slope).astype(BF16)
     gather(pg, a_rows, acts_at, "ag_b", chip_peer, chips)
 
+    proj[ring_own, :] = ring_total("p", pp, pp_f, pp_n, v_rows).astype(BF16)
+    ring_gather("p", proj, v_rows)
     ring_forward("p", proj, v_rows)
 
     wait_for(pg.at[pl.ds(0, (chips - 1) * a_rows)], "ag_b")
@@ -384,56 +395,64 @@
     wait_for(pg.at[twin_half], "back_b")
     px[...] = dot_nn(h_t[...], pg[...])
     px_s[...] = px[...].astype(px_s.dtype)
-    ring_scatter("g", px_s, px_r, v_rows)
+    ring_scatter("g", px, px_s, px_r, px_n, v_rows)
 
     ring_done("p", proj, v_rows)
     up = dot_nt(proj[...], hw[...])
     for side in range(2):
         pc[side] = up[:, side * half_w:(side + 1) * half_w]
-    remote(pc.at[other], pair_c, "pair_c", twin_id).start()
-    wait_for(pair_c, "pair_c")
-    pc2[...] = (pc[core] + pair_c[...]).astype(pc2.dtype)
-    scatter(pc2, c_rows, rv_c, "rs_c", chip_peer, chip, chips)
-
-    ring_relay("g", px, px_o, px_r, v_rows)
-    gag[ring_own, :] = ring_total("g", px, px_r, v_rows).astype(gag.dtype)
+        pc_s[side] = up[:, side * half_w:(side + 1) * half_w].astype(pc_s.dtype)
+
+    def c_block(ref, device):
+        return ref.at[device % 2, pl.ds(pl.multiple_of(device // 2 * c_rows, c_rows), c_rows)]
+
+    def send_c(index):
+        offset = ordered(index, n_voc)
+        target = lax.rem(v + offset, n_voc)
+        remote(c_block(pc_s, target), rv_c.at[offset - 1], "rs_c", voc_peer(offset)).start()
+    loop(n_voc - 1, send_c)
+
+    ring_relay("g", px, px_o, px_f, px_r, v_rows)
+    gag[ring_own, :] = ring_total("g", px, px_f, px_n, v_rows).astype(gag.dtype)
     ring_gather("g", gag, v_rows)
 
-    own_c = pl.ds(pl.multiple_of(chip * c_rows, c_rows), c_rows)
     wait_for(rv_c, "rs_c")
-    gcol[own_c, :] = total(pc2[own_c, :].astype(F32), rv_c, chips).astype(gcol.dtype)
-    gather(gcol, c_rows, chip * c_rows, "ag_c", chip_peer, chips)
+    c_block(gall, v)[...] = total(c_block(pc, v)[...], rv_c, n_voc).astype(gall.dtype)
+
+    def share_c(index):
+        block = c_block(gall, v)
+        remote(block, block, "ag_c", voc_peer(ordered(index, n_voc))).start()
+    loop(n_voc - 1, share_c)
     ring_forward("g", gag, v_rows)
-    wait_for(gcol.at[pl.ds(0, (chips - 1) * c_rows)], "ag_c")
-    remote(gcol, gpart, "back_c", twin_id).start()
-
     ring_done("g", gag, v_rows)
-    ga_ref[...] = gag[...].astype(F32)
-    wait_for(gpart, "back_c")
-
-    mine = gcol[...].astype(F32)
-    theirs = gpart[...].astype(F32)
-    gb_ref[:, :half_w] = jnp.where(core == 0, mine, theirs)
-    gb_ref[:, half_w:] = jnp.where(core == 0, theirs, mine)
+    ga_ref[...] = gag[...]
+    wait_for(rv_c, "ag_c")
+    gb_ref[...] = gall[...]
 
     wait_sent(t.at[pl.ds(rows, 8)], "halo")
     wait_sent(pair_a, "pair_a")
     wait_sent(rv_a, "rs_a")
     wait_sent(acts.at[pl.ds(0, (chips - 1) * a_rows)], "ag_a")
     wait_sent(acts.at[mine_half], "back_a")
-    ring_sent("v", pv_r, vp, v_rows)
+    ring_sent("v", pv_f, pv_r, pv_n, vp, v_rows)
     for offset in range(1, per_book):
         wait_sent(stat, f"s{offset}")
     wait_sent(pair_b, "pair_b")
     wait_sent(rv_b, "rs_b")
     wait_sent(pg.at[pl.ds(0, (chips - 1) * a_rows)], "ag_b")
     wait_sent(pg.at[mine_half], "back_b")
-    ring_sent("p", pp_r, proj, v_rows)
-    ring_sent("g", px_r, gag, v_rows)
-    wait_sent(pair_c, "pair_c")
+    ring_sent("p", pp_f, pp_r, pp_n, proj, v_rows)
+    ring_sent("g", px_f, px_r, px_n, gag, v_rows)
     wait_sent(rv_c, "rs_c")
-    wait_sent(gcol.at[pl.ds(0, (chips - 1) * c_rows)], "ag_c")
-    wait_sent(gcol, "back_c")
+    wait_sent(rv_c, "ag_c")
+
+
+def finish(loss_ref, ga_ref, gb_ref, loss_out, ga_out, gb_out):
+    half_w = gb_ref.shape[2]
+    loss_out[...] = loss_ref[...]
+    ga_out[...] = ga_ref[...].astype(F32)
+    for side in range(2):
+        gb_out[:, side * half_w:(side + 1) * half_w] = gb_ref[side].astype(F32)
 
 
 def on_device(n_grp, n_voc, hidden_states, target_logits, labels, down_weight, up_weight, head_weight):
@@ -452,45 +471,57 @@
     vm = pltpu.VMEM
     w = WIRE
     scratch = [
-        vm((rows, deep), BF16), vm((rows + 8, width), F32), vm((deep, rank), BF16),
+        vm((rows, deep), BF16), vm((rows + 8, width), F32), vm((n_book, rows), jnp.int32), vm((deep, rank), BF16),
         vm((rank, span), BF16), vm((span, width), BF16), vm((deep, rows), BF16),
-        vm((rank, width), F32), vm((rank, width), w["v"]), vm((2, v_rows, width), w["v"]),
-        vm((4 * HOP - 1, v_rows, width), w["v"]), vm((rank, width), BF16),
+        vm((rank, width), F32), vm((rank, width), w["v"]), vm((2, v_rows, width), w["vx"]),
+        vm((2, v_rows, width), w["vx"]), vm((2 * HOP - 2, v_rows, width), w["vn"]),
+        vm((2 * HOP - 1, v_rows, width), w["v"]), vm((rank, width), BF16),
         vm((rows, rank), F32), vm((half, rank), F32),
         vm((half, rank), w["a"]), vm((chips - 1, a_rows, rank), w["a"]), vm((a_rows, rank), F32),
         vm((rows, rank), BF16), vm((rank, rows), BF16),
         vm((rows, 128), F32), vm((rows, width), F32), vm((rows, width), F32),
         vm((rows, width), F32), vm((rows, 128), F32), vm((8, rows), F32),
         vm((per_book - 1, 8, rows), F32), vm((128, rows), F32), vm((rows, width), BF16),
-        vm((rank, width), F32), vm((rank, width), w["p"]), vm((2, v_rows, width), w["p"]),
-        vm((4 * HOP - 1, v_rows, width), w["p"]), vm((rank, width), BF16),
+        vm((rank, width), F32), vm((rank, width), w["p"]), vm((2, v_rows, width), w["px"]),
+        vm((2, v_rows, width), w["px"]), vm((2 * HOP - 2, v_rows, width), w["pn"]),
+        vm((2 * HOP - 1, v_rows, width), w["p"]), vm((rank, width), BF16),
         vm((rows, rank), F32), vm((half, rank), F32),
         vm((half, rank), w["b"]), vm((chips - 1, a_rows, rank), w["b"]), vm((rows, rank), BF16),
-        vm((deep, rank), F32), vm((deep, rank), w["g"]), vm((2, v_rows, rank), w["g"]),
-        vm((4 * HOP - 1, v_rows, rank), w["g"]), vm((deep, rank), w["ag"]),
-        vm((2, rank, half_w), F32), vm((rank, half_w), F32),
-        vm((rank, half_w), w["c"]), vm((chips - 1, c_rows, half_w), w["c"]), vm((rank, half_w), w["ac"]),
-        vm((rank, half_w), w["ac"]),
-        pltpu.SemaphoreType.DMA((5,)),
+        vm((deep, rank), F32), vm((deep, rank), w["g"]), vm((2, v_rows, rank), w["gx"]),
+        vm((2, v_rows, rank), w["gx"]), vm((2 * HOP - 2, v_rows, rank), w["gn"]),
+        vm((2 * HOP - 1, v_rows, rank), w["g"]), vm((deep, rank), w["ga"]),
+        vm((2, rank, half_w), F32), vm((2, rank, half_w), w["c"]),
+        vm((n_voc - 1, c_rows, half_w), w["c"]), vm((2, rank, half_w), w["c"]),
+        pltpu.SemaphoreType.DMA((6,)),
         pltpu.SemaphoreType.DMA((len(PHASES),)),
         pltpu.SemaphoreType.DMA((len(PHASES),)),
     ]
     hbm = pl.BlockSpec(memory_space=pl.ANY)
     vmem = pl.BlockSpec(memory_space=pltpu.VMEM)
+    parts = pl.pallas_call(
+        functools.partial(kernel, n_grp, n_voc, n_book),
+        out_shape=(
+            jax.ShapeDtypeStruct((1, 1, rows // per_book), F32),
+            jax.ShapeDtypeStruct((deep, rank), w["ga"]),
+            jax.ShapeDtypeStruct((2, rank, half_w), w["c"]),
+        ),
+        in_specs=[hbm] * 6,
+        out_specs=(vmem, vmem, vmem),
+        scratch_shapes=scratch,
+        compiler_params=pltpu.CompilerParams(
+            collective_id=0, has_side_effects=True, vmem_limit_bytes=56 * 1024 * 1024
+        ),
+    )(hidden_states, target_logits, labels.T, down_weight, up_weight, head_weight)
     return pl.pallas_call(
-        functools.partial(kernel, n_grp, n_voc, n_book),
+        finish,
         out_shape=(
             jax.ShapeDtypeStruct((1, 1, rows // per_book), F32),
             jax.ShapeDtypeStruct((deep, rank), F32),
             jax.ShapeDtypeStruct((rank, span), F32),
         ),
-        in_specs=[hbm, hbm, vmem, hbm, hbm, hbm],
+        in_specs=[vmem] * 3,
         out_specs=(vmem, vmem, vmem),
-        scratch_shapes=scratch,
-        compiler_params=pltpu.CompilerParams(
-            collective_id=0, has_side_effects=True, vmem_limit_bytes=60 * 1024 * 1024
-        ),
-    )(hidden_states, target_logits, labels, down_weight, up_weight, head_weight)
+    )(*parts)
 
 
 def solution(mesh):

time: 95.6 us -> 89.5 us (0.936)
  local copies, waits for them, and re-layouts: 6.52 us -> 0 us
    unnamed x4 -> x0, local copies, waits for them, and re-layouts: 6.52 us -> none
    pallas_call x0 -> x1, Pallas kernels: none -> 1.94 us  [on_device(): pl.pallas_call(finish, out_shape=(jax.ShapeDtypeStruct((1, 1, rows // per...]
    pallas_call x1, Pallas kernels: 88.1 us -> 86.8 us  [on_device(): pl.pallas_call(functools.partial(kernel, n_grp, n_voc, n_book), out_shape...]
where the time goes in v2:
time: 89.5 us; the launch traced here: 89.4 us
  Pallas kernels  88.7 us (99%)
    pallas_call x1, Pallas kernels, on_device(): pl.pallas_call(functools.partial(kernel, n_grp, n_voc, n_book), out_shape...  86.8 us
    pallas_call x1, Pallas kernels, on_device(): pl.pallas_call(finish, out_shape=(jax.ShapeDtypeStruct((1, 1, rows // per...  1.94 us

profile of v2, /device:TPU:2, one launch (start us, length us, event | category | flops | bytes accessed | tf_op | source)
XLA Modules:
  0.0 89.4 jit_solution(5823221233117488977)
XLA Ops:
  0.6 86.8 %shard_map.85 = (f32[1,1,256]{2,1,0:T(1,128)}, f32[256,256]{1,0:T(8,128)}, bf16[2,256,256]{2,1,0:T(8,128)(2,1)}) custom-call(bf16[1024,256]{1,0:T(8,128)(2,1)} %h_any.1, f32[1024,512]{1,0:T(8,128)} %t_any.1, s32[8,1024]{1,0:T(8,128)} %bitcast.1, bf16[256,256]{1,0:T(8,128)(2,1)} %dw_any.1, bf16[256,512]{1,0:T(8,128)(2,1)} %uw_any.1, bf16[512,512]{1,0:T(8,128)(2,1)} %hw_any.1), custom_call_target="tpu_custom_call" | custom-call | tf_op jit(solution)/shard_map/pallas_call | solution.py:501
  87.5 1.9 %shard_map.86 = (f32[1,1,256]{2,1,0:T(1,128)}, f32[256,256]{1,0:T(8,128)}, f32[256,512]{1,0:T(8,128)}) custom-call(f32[1,1,256]{2,1,0:T(1,128)} %get-tuple-element.6.loss_ref, f32[256,256]{1,0:T(8,128)} %get-tuple-element.7.ga_ref, bf16[2,256,256]{2,1,0:T(8,128)(2,1)} %get-tuple-element.8.gb_ref), custom_call_target="tpu_custom_call" | custom-call | tf_op jit(solution)/shard_map/pallas_call | solution.py:515

commit v3 on v2

--- a/solution.py
+++ b/solution.py
@@ -15,11 +15,11 @@
 CHUNK = 128
 WIRE = {
     "a": F32, "b": F32, "c": BF16, "v": BF16, "vn": BF16, "vx": F32,
-    "p": BF16, "pn": BF16, "px": BF16, "g": BF16, "gn": BF16, "gx": BF16, "ga": F32,
+    "p": BF16, "pn": BF16, "px": BF16, "g": BF16, "gn": BF16, "gx": BF16, "ga": BF16,
 }
 
 PHASES = (
-    "halo", "pair_a", "rs_a", "ag_a", "back_a", "s1", "s2", "s3",
+    "halo", "pair_a", "rs_a", "ag_a", "back_a", "s01", "s02", "s03", "s11", "s12", "s13",
     "pair_b", "rs_b", "ag_b", "back_b", "rs_c", "ag_c",
 ) + tuple(
     ring + stage
@@ -226,25 +226,25 @@
     loads[1].wait()
     pv[...] = dot_nn(uw[...], hw[...])
     pv_s[...] = pv[...].astype(pv_s.dtype)
+    loads[2].wait()
+    loads[3].wait()
+
+    mine_half = pl.ds(pl.multiple_of(core * half, half), half)
+    twin_half = pl.ds(pl.multiple_of(other * half, half), half)
+    twin_id = {"grp": g, "voc": twin}
+
+    def half_dots(dst, start, left, dot, right):
+        def body(index):
+            at = pl.ds(pl.multiple_of(start + index * 256, 256), 256)
+            dst[at, :] = dot(left[at, :], right[...])
+        loop(half // 256, body)
+
+    half_dots(pa, other * half, h, dot_nn, dw)
     pl.semaphore_wait(barrier, 2 * HOP + n_voc - 1)
     ring_scatter("v", pv, pv_s, pv_r, pv_n, v_rows)
     remote(
         t_any.at[pl.ds(0, 8)], t.at[pl.ds(rows, 8)], "halo", ring_peer(-1)
     ).start()
-    loads[2].wait()
-    loads[3].wait()
-
-    mine_half = pl.ds(pl.multiple_of(core * half, half), half)
-    twin_half = pl.ds(pl.multiple_of(other * half, half), half)
-    twin_id = {"grp": g, "voc": twin}
-
-    def half_dots(dst, start, left, dot, right):
-        def body(index):
-            at = pl.ds(pl.multiple_of(start + index * 256, 256), 256)
-            dst[at, :] = dot(left[at, :], right[...])
-        loop(half // 256, body)
-
-    half_dots(pa, other * half, h, dot_nn, dw)
 
     remote(pa.at[twin_half], pair_a, "pair_a", twin_id).start()
     half_dots(pa, core * half, h, dot_nn, dw)
@@ -306,9 +306,9 @@
         col = lax.broadcasted_iota(jnp.int32, (CHUNK, 128), 1).astype(F32)
         return jnp.concatenate([labels == col + 128.0 * k for k in range(width // 128)], 1)
 
-    def draft_pass(index):
-        start = pl.multiple_of(index * CHUNK, CHUNK)
-        at = pl.ds(start, CHUNK)
+    def draft_pass(side, index):
+        local = pl.ds(pl.multiple_of(index * CHUNK, CHUNK), CHUNK)
+        at = pl.ds(pl.multiple_of(side * half + index * CHUNK, CHUNK), CHUNK)
         draft = t[at, :] + dot_nn(acts[at, :], vp[...])
         top = jnp.max(draft, -1, keepdims=True)
         low = draft - top
@@ -323,42 +323,42 @@
         cols = jnp.where(lane == 3, norm, cols)
         cols = jnp.where(lane == 4, cross, cols)
         cols = jnp.where(lane == 5, picked, cols)
-        stat[:, at] = cols.T[:8]
+        stat[side, :, local] = cols.T[:8]
+    wait_for(acts.at[twin_half], "back_a")
     steps = half // CHUNK
-    loop(steps, lambda index: draft_pass(core * steps + index))
-    wait_for(acts.at[twin_half], "back_a")
-    loop(steps, lambda index: draft_pass(other * steps + index))
-
-    for offset in range(1, per_book):
-        remote(stat, rv_s.at[offset - 1], f"s{offset}", book_peer(offset)).start()
+    for side in range(2):
+        loop(steps, functools.partial(draft_pass, side))
+        for offset in range(1, per_book):
+            remote(
+                stat.at[side], rv_s.at[side, offset - 1], f"s{side}{offset}", book_peer(offset)
+            ).start()
     turn(acts, acts_t)
-    for offset in range(1, per_book):
-        wait_for(rv_s.at[offset - 1], f"s{offset}")
-
-    blocks = [stat[...]] + [rv_s[k] for k in range(per_book - 1)]
 
     def row(block, k):
         return block[k:k + 1, :]
 
-    top_t = functools.reduce(jnp.maximum, [row(b, 0) for b in blocks])
-    top_d = functools.reduce(jnp.maximum, [row(b, 2) for b in blocks])
-    fac_t = [jnp.exp(row(b, 0) - top_t) for b in blocks]
-    fac_d = [jnp.exp(row(b, 2) - top_d) for b in blocks]
-    sum_t = sum(row(b, 1) * f for b, f in zip(blocks, fac_t))
-    sum_d = sum(row(b, 3) * f for b, f in zip(blocks, fac_d))
-    cross = sum(
-        f * (row(b, 4) + row(b, 1) * ((row(b, 0) - top_t) - (row(b, 2) - top_d)))
-        for b, f in zip(blocks, fac_t)
-    )
-    picked = sum(row(b, 5) for b in blocks) - top_d - jnp.log(sum_d)
-    frame = g * rows + lax.broadcasted_iota(jnp.int32, (1, rows), 1)
-    live = (frame < rows * n_grp - HEAD).astype(F32)
-    diverge = cross / sum_t - jnp.log(sum_t) + jnp.log(sum_d)
-    comb[0:1, :] = (live + LAM) * fac_d[0] / sum_d
-    comb[1:2, :] = live * fac_t[0] / sum_t
-    comb[2:3, :] = live * diverge - LAM * picked
-    block_rows = rows // per_book
-    loss_ref[0] = comb[2:3, pl.ds(pl.multiple_of(part * block_rows, block_rows), block_rows)]
+    def combine(side):
+        for offset in range(1, per_book):
+            wait_for(rv_s.at[side, offset - 1], f"s{side}{offset}")
+        blocks = [stat[side]] + [rv_s[side, k] for k in range(per_book - 1)]
+        top_t = functools.reduce(jnp.maximum, [row(b, 0) for b in blocks])
+        top_d = functools.reduce(jnp.maximum, [row(b, 2) for b in blocks])
+        fac_t = [jnp.exp(row(b, 0) - top_t) for b in blocks]
+        fac_d = [jnp.exp(row(b, 2) - top_d) for b in blocks]
+        sum_t = sum(row(b, 1) * f for b, f in zip(blocks, fac_t))
+        sum_d = sum(row(b, 3) * f for b, f in zip(blocks, fac_d))
+        cross = sum(
+            f * (row(b, 4) + row(b, 1) * ((row(b, 0) - top_t) - (row(b, 2) - top_d)))
+            for b, f in zip(blocks, fac_t)
+        )
+        picked = sum(row(b, 5) for b in blocks) - top_d - jnp.log(sum_d)
+        frame = g * rows + side * half + lax.broadcasted_iota(jnp.int32, (1, half), 1)
+        live = (frame < rows * n_grp - HEAD).astype(F32)
+        diverge = cross / sum_t - jnp.log(sum_t) + jnp.log(sum_d)
+        at = pl.ds(side * half, half)
+        comb[0:1, at] = (live + LAM) * fac_d[0] / sum_d
+        comb[1:2, at] = live * fac_t[0] / sum_t
+        comb[2:3, at] = live * diverge - LAM * picked
 
     def grad_pass(index):
         at = pl.ds(pl.multiple_of(index * CHUNK, CHUNK), CHUNK)
@@ -366,19 +366,25 @@
         value = ed[at, :] * cols[:, 0:1] - et[at, :] * cols[:, 1:2]
         value = value - jnp.where(label_mask(at), LAM, 0.0)
         grad[at, :] = value.astype(BF16)
-    loop(rows // CHUNK, grad_pass)
-
+    for side in range(2):
+        combine(side)
+        loop(steps, lambda index: grad_pass(side * steps + index))
+    block_rows = rows // per_book
+    loss_ref[0] = comb[2:3, pl.ds(pl.multiple_of(part * block_rows, block_rows), block_rows)]
+
+    half_dots(pb, other * half, grad, dot_nt, vp)
+    remote(pb.at[twin_half], pair_b, "pair_b", twin_id).start()
     pp[...] = dot_nn(acts_t[...], grad[...])
     pp_s[...] = pp[...].astype(pp_s.dtype)
     ring_scatter("p", pp, pp_s, pp_r, pp_n, v_rows)
 
-    half_dots(pb, other * half, grad, dot_nt, vp)
-    remote(pb.at[twin_half], pair_b, "pair_b", twin_id).start()
     half_dots(pb, core * half, grad, dot_nt, vp)
     wait_for(pair_b, "pair_b")
     pb2[...] = (pb[mine_half, :] + pair_b[...]).astype(pb2.dtype)
     scatter(pb2, a_rows, rv_b, "rs_b", chip_peer, chip, chips)
     ring_relay("p", pp, pp_o, pp_f, pp_r, v_rows)
+    proj[ring_own, :] = ring_total("p", pp, pp_f, pp_n, v_rows).astype(BF16)
+    ring_gather("p", proj, v_rows)
     wait_for(rv_b, "rs_b")
     act_grad = total(pb2[own_a, :].astype(F32), rv_b, chips)
     sigma = 1.0 / (1.0 + jnp.exp(-pre[...]))
@@ -386,14 +392,13 @@
     pg[pl.ds(pl.multiple_of(acts_at, a_rows), a_rows), :] = (act_grad * slope).astype(BF16)
     gather(pg, a_rows, acts_at, "ag_b", chip_peer, chips)
 
-    proj[ring_own, :] = ring_total("p", pp, pp_f, pp_n, v_rows).astype(BF16)
-    ring_gather("p", proj, v_rows)
     ring_forward("p", proj, v_rows)
 
     wait_for(pg.at[pl.ds(0, (chips - 1) * a_rows)], "ag_b")
     remote(pg.at[mine_half], pg.at[mine_half], "back_b", twin_id).start()
+    px[...] = dot_nn(h_t[:, mine_half], pg[mine_half, :])
     wait_for(pg.at[twin_half], "back_b")
-    px[...] = dot_nn(h_t[...], pg[...])
+    px[...] = px[...] + dot_nn(h_t[:, twin_half], pg[twin_half, :])
     px_s[...] = px[...].astype(px_s.dtype)
     ring_scatter("g", px, px_s, px_r, px_n, v_rows)
 
@@ -435,8 +440,9 @@
     wait_sent(acts.at[pl.ds(0, (chips - 1) * a_rows)], "ag_a")
     wait_sent(acts.at[mine_half], "back_a")
     ring_sent("v", pv_f, pv_r, pv_n, vp, v_rows)
-    for offset in range(1, per_book):
-        wait_sent(stat, f"s{offset}")
+    for side in range(2):
+        for offset in range(1, per_book):
+            wait_sent(stat.at[side], f"s{side}{offset}")
     wait_sent(pair_b, "pair_b")
     wait_sent(rv_b, "rs_b")
     wait_sent(pg.at[pl.ds(0, (chips - 1) * a_rows)], "ag_b")
@@ -480,8 +486,8 @@
         vm((half, rank), w["a"]), vm((chips - 1, a_rows, rank), w["a"]), vm((a_rows, rank), F32),
         vm((rows, rank), BF16), vm((rank, rows), BF16),
         vm((rows, 128), F32), vm((rows, width), F32), vm((rows, width), F32),
-        vm((rows, width), F32), vm((rows, 128), F32), vm((8, rows), F32),
-        vm((per_book - 1, 8, rows), F32), vm((128, rows), F32), vm((rows, width), BF16),
+        vm((rows, width), F32), vm((rows, 128), F32), vm((2, 8, half), F32),
+        vm((2, per_book - 1, 8, half), F32), vm((128, rows), F32), vm((rows, width), BF16),
         vm((rank, width), F32), vm((rank, width), w["p"]), vm((2, v_rows, width), w["px"]),
         vm((2, v_rows, width), w["px"]), vm((2 * HOP - 2, v_rows, width), w["pn"]),
         vm((2 * HOP - 1, v_rows, width), w["p"]), vm((rank, width), BF16),
@@ -501,9 +507,9 @@
     parts = pl.pallas_call(
         functools.partial(kernel, n_grp, n_voc, n_book),
         out_shape=(
-            jax.ShapeDtypeStruct((1, 1, rows // per_book), F32),
-            jax.ShapeDtypeStruct((deep, rank), w["ga"]),
-            jax.ShapeDtypeStruct((2, rank, half_w), w["c"]),
+            vm((1, 1, rows // per_book), F32),
+            vm((deep, rank), w["ga"]),
+            vm((2, rank, half_w), w["c"]),
         ),
         in_specs=[hbm] * 6,
         out_specs=(vmem, vmem, vmem),
@@ -521,7 +527,8 @@
         ),
         in_specs=[vmem] * 3,
         out_specs=(vmem, vmem, vmem),
-    )(*parts)
+        compiler_params=pltpu.CompilerParams(vmem_limit_bytes=4 * 1024 * 1024),
+    )(*[pltpu.with_memory_space_constraint(part, pltpu.VMEM) for part in parts])
 
 
 def solution(mesh):

time: 89.5 us -> 85.6 us (0.956)
  the two profiles are of different devices: /device:TPU:2 before, /device:TPU:8 now
where the time goes in v3:
time: 85.6 us; the launch traced here: 85.5 us
  Pallas kernels  84.8 us (99%)
    pallas_call x1, Pallas kernels, on_device(): pl.pallas_call(functools.partial(kernel, n_grp, n_voc, n_book), out_shape...  83.9 us

profile of v3, /device:TPU:8, one launch (start us, length us, event | category | flops | bytes accessed | tf_op | source)
XLA Modules:
  0.0 85.5 jit_solution(14481297070847369679)
XLA Ops:
  0.6 83.9 %shard_map.85 = (f32[1,1,256]{2,1,0:T(1,128)S(1)}, bf16[256,256]{1,0:T(8,128)(2,1)S(1)}, bf16[2,256,256]{2,1,0:T(8,128)(2,1)S(1)}) custom-call(bf16[1024,256]{1,0:T(8,128)(2,1)} %h_any.1, f32[1024,512]{1,0:T(8,128)} %t_any.1, s32[8,1024]{1,0:T(8,128)} %bitcast.1, bf16[256,256]{1,0:T(8,128)(2,1)} %dw_any.1, bf16[256,512]{1,0:T(8,128)(2,1)} %uw_any.1, ...), custom_call_target="tpu_custom_call" | custom-call | tf_op jit(solution)/shard_map/pallas_call | solution.py:507
  84.6 0.9 %shard_map.86 = (f32[1,1,256]{2,1,0:T(1,128)}, f32[256,256]{1,0:T(8,128)}, f32[256,512]{1,0:T(8,128)}) custom-call(f32[1,1,256]{2,1,0:T(1,128)S(1)} %get-tuple-element.6.loss_ref, bf16[256,256]{1,0:T(8,128)(2,1)S(1)} %get-tuple-element.7.ga_ref, bf16[2,256,256]{2,1,0:T(8,128)(2,1)S(1)} %get-tuple-element.8.gb_ref), custom_call_target="tpu_custom_call" | custom-call | tf_op jit(solution)/shard_map/pallas_call | solution.py:521
